TPU v7x, 256 devices: a whole 4x4x8 slice. The times are simulated.
256 devices in a mesh: occ: 16 (over z_hi, y, core), vir: 16 (over z_lo, x).
Axes of the slice: x: 4, y: 4, z: 8 (z_hi: 2, z_lo: 4; z = z_hi * 4 + z_lo), core: 2. Of those that a mesh axis runs over, the one named last changes fastest.
Arguments:
- amplitudes: bfloat16 [8192, 8192], P('occ', 'vir'), may hold values from -6 to 6
- hole_integrals: bfloat16 [8192, 8192], P('occ'), may hold values from -0.1875 to 0.1875
- particle_integrals: bfloat16 [8192, 8192], P('vir'), may hold values from -0.25 to 0.25
- occ_irrep: int32 [128], replicated, may hold values from 0 to 7
- vir_irrep: int32 [128], replicated, may hold values from 0 to 7
- occ_energy: float32 [8192], P('occ'), may hold values from -1.5 to -0.5
- vir_energy: float32 [8192], P('vir'), may hold values from 0.5 to 2.5
Outputs:
- update: float32 [8192, 8192], P('vir', 'occ')
All inputs are finite; a program needn't handle non-finite values.
Results may differ from a plain program's by a relative error of at most 0.0003.
Values may be sent and summed in bfloat16 or wider, within the bound.
No kernel may reach another device: no remote copies, remote signals or barrier semaphores. Data moves between devices by JAX's collectives and lax.ppermute only.
A program may use at most 128 MiB of HBM per device.

v0:
```python
import jax
import jax.numpy as jnp
from jax import lax
from jax.sharding import PartitionSpec as P

TILE = 64


def per_device(
    amplitudes, hole_integrals, particle_integrals, occ_irrep, vir_irrep, occ_energy, vir_energy
):
    own_rows = amplitudes.shape[0]
    own_pairs = amplitudes.shape[1]
    zero_value = jnp.zeros((), jnp.bfloat16)
    occ_labels = jnp.repeat(occ_irrep, TILE)
    vir_labels = jnp.repeat(vir_irrep, TILE)
    own_occ = lax.dynamic_slice_in_dim(occ_labels, lax.axis_index("occ") * own_rows, own_rows)
    own_vir = lax.dynamic_slice_in_dim(vir_labels, lax.axis_index("vir") * own_pairs, own_pairs)
    hole_masked = jnp.where(own_occ[:, None] == occ_labels[None, :], hole_integrals, zero_value)
    contract_first = (((0,), (1,)), ((), ()))
    hole = lax.dot_general(
        lax.all_gather(amplitudes, "occ", axis=0, tiled=True),
        hole_masked,
        contract_first,
        preferred_element_type=jnp.float32,
    )
    slab_masked = jnp.where(own_vir[:, None] == vir_labels[None, :], particle_integrals, zero_value)
    particle = lax.psum_scatter(
        lax.dot_general(
            slab_masked, amplitudes, contract_first, preferred_element_type=jnp.float32
        ),
        "vir",
        scatter_dimension=0,
        tiled=True,
    )
    energy_gap = vir_energy[:, None] - occ_energy[None, :]
    return (hole + particle) / energy_gap


def solution(mesh):
    placed = (P("occ", "vir"), P("occ", None), P("vir", None), P(), P(), P("occ"), P("vir"))
    return jax.shard_map(
        per_device, mesh=mesh, in_specs=placed, out_specs=P("vir", "occ"), check_vma=False
    )
```

profile of v0, /device:TPU:65, one launch (start us, length us, event | category | flops | bytes accessed | tf_op | source)
XLA Modules:
  0.0 290.1 jit_solution(7640333086408449033)
XLA Ops:
  7.4 0.0 all-gather.2.cloned.1.call-start
  7.4 0.7 all-gather.2.cloned.1.call-update
  8.1 0.0 reduce-scatter.2.cloned.1.call-start
  8.1 0.7 broadcast_in_dim.17
  8.9 0.1 reshape.13
  9.0 0.1 dynamic_slice.7
  9.0 14.0 %fusion.1 = f32[8192,512]{0,1:T(8,128)} fusion(bf16[512,512]{1,0:T(8,128)(2,1)} %param.7, bf16[512,8192]{1,0:T(8,128)(2,1)} %param.9, s32[8192]{0:T(1024)S(1)} %reshape.13, s32[512]{0:T(512)S(1)} %dynamic_slice.7), kind=kOutput, calls=%fused_computation.3 | convolution fusion | flops 4303355904 | bytes 25724928 | tf_op jit(solution)/shard_map/dot_general | solution.py:29
  23.0 0.0 copy-start
  23.0 0.0 copy-start.1
  23.0 0.0 copy-start.2
  23.0 0.0 reduce-scatter.2.cloned.1.call-update
  23.0 0.6 copy-done
  23.7 0.1 broadcast_in_dim.15
  23.7 0.1 reshape.12
  23.8 0.1 dynamic_slice.6
  23.9 246.9 %all-gather.2.cloned.1.call-done = bf16[8192,512]{1,0:T(8,128)(2,1)} async-done(((bf16[512,512]{1,0:T(8,128)(2,1)}), bf16[8192,512]{1,0:T(8,128)(2,1)}) %all-gather.2.cloned.1.call-update) | async-done | bytes 8388624 | tf_op jit(solution)/shard_map/all_gather | solution.py:22
  270.8 0.0 reduce-scatter.2.cloned.1.call-done
  270.8 0.0 copy-done.1
  270.8 0.0 copy-done.2
  270.8 10.5 %subtract_divide_fusion = f32[512,512]{0,1:T(8,128)S(1)} fusion(f32[512,512]{0,1:T(8,128)} %reduce-scatter.2.cloned.1.call-done, bf16[8192,512]{1,0:T(8,128)(2,1)} %all-gather.2.cloned.1.call-done, bf16[512,8192]{1,0:T(8,128)(2,1)} %param.8, s32[8192]{0:T(1024)S(1)} %reshape.12, s32[512]{0:T(512)S(1)} %dynamic_slice.6, f32[512]{0:T(512)S(1)} %copy-done.1, ...), kind=kOutput, calls=%fused_computation.12 | convolution fusion | flops 4304142336 | bytes 18913280 | tf_op jit(solution)/shard_map/dot_general | solution.py:21
  281.3 1.3 copy.11
Async XLA Ops:
  7.4 263.4 %all-gather.2.cloned.1.call-start = ((), (), s32[]{:S(2)}) async-start(), calls=%async_computation.1 | async-start | bytes 8912896 | tf_op jit(solution)/shard_map/all_gather | solution.py:22
  8.1 262.7 %reduce-scatter.2.cloned.1.call-start = ((), (), s32[]{:S(2)}) async-start(), calls=%async_computation.2 | async-start | bytes 17825792 | tf_op jit(solution)/shard_map/reduce_scatter | solution.py:28
  23.0 0.7 copy-start
  23.0 247.8 %copy-start.1 = (f32[512]{0:T(512)S(1)}, f32[512]{0:T(512)}, u32[]{:S(2)}) copy-start(f32[512]{0:T(512)} %param.12) | copy-start | bytes 6148
  23.0 247.8 %copy-start.2 = (f32[512]{0:T(512)S(1)}, f32[512]{0:T(512)}, u32[]{:S(2)}) copy-start(f32[512]{0:T(512)} %param.13) | copy-start | bytes 6148
Sparse Core Ops, SparseCore 0:
  10.9 259.8 all-gather.1
Sparse Core Ops, SparseCore 1:
  23.1 234.3 reduce-scatter.1
where the time goes:
time: 290 us
  waiting for transfers between devices  248 us (86%)
  matrix products  24.5 us (8%)
  between operations  14.9 us (5%)
  local copies, waits for them, and re-layouts  3.04 us (1%)
    all_gather x1, waiting for transfers between devices, per_device(): lax.all_gather(amplitudes, 'occ', axis=0, tiled=True)  247 us
    dot_general x1, matrix products, per_device(): lax.dot_general(slab_masked, amplitudes, contract_first, preferred_elemen...  14 us
    dot_general x1, matrix products, per_device(): lax.dot_general(lax.all_gather(amplitudes, 'occ', axis=0, tiled=True), ho...  10.5 us
  transfers between devices with their start and end apart: 2, of which 1 were waited for; matrix products, arithmetic and copies ran while one was open for 5% of the time, Pallas kernels for 0%

commit v1 on v0

--- a/solution.py
+++ b/solution.py
@@ -4,6 +4,13 @@
 from jax.sharding import PartitionSpec as P
 
 TILE = 64
+
+
+def open_paths_over_axis(panel, k_dim):
+    tmp = jnp.stack([panel] * jax.lax.axis_size("occ"))
+    seen_now = jax.lax.all_to_all(tmp, "occ", 0, 0)
+    tile_out = jnp.concatenate(seen_now, axis=k_dim)
+    return tile_out
 
 
 def per_device(
@@ -19,7 +26,7 @@
     hole_masked = jnp.where(own_occ[:, None] == occ_labels[None, :], hole_integrals, zero_value)
     contract_first = (((0,), (1,)), ((), ()))
     hole = lax.dot_general(
-        lax.all_gather(amplitudes, "occ", axis=0, tiled=True),
+        open_paths_over_axis(amplitudes, 0),
         hole_masked,
         contract_first,
         preferred_element_type=jnp.float32,

time: 290 us -> 441 us (1.52)
  the two profiles are of different devices: /device:TPU:65 before, /device:TPU:8 now
where the time goes in v1:
time: 441 us
  waiting for transfers between devices  384 us (87%)
  matrix products  24.5 us (6%)
  between operations  13.4 us (3%)
  starting transfers between devices  11.7 us (3%)
  local copies, waits for them, and re-layouts  7.48 us (2%)
    reduce_scatter x1, waiting for transfers between devices, per_device(): lax.psum_scatter(lax.dot_general(slab_masked, amplitudes, contract_first,...  202 us
    all_to_all x1, waiting for transfers between devices, open_paths_over_axis(): seen_now = jax.lax.all_to_all(tmp, 'occ', 0, 0)  182 us
    dot_general x1, matrix products, per_device(): lax.dot_general(slab_masked, amplitudes, contract_first, preferred_elemen...  14 us
    all_to_all x1, starting transfers between devices, open_paths_over_axis(): seen_now = jax.lax.all_to_all(tmp, 'occ', 0, 0)  11.7 us
    dot_general x1, matrix products, per_device(): lax.dot_general(open_paths_over_axis(amplitudes, 0), hole_masked, contrac...  10.5 us
  transfers between devices with their start and end apart: 2, of which 2 were waited for; matrix products, arithmetic and copies ran while one was open for 1% of the time, Pallas kernels for 0%

profile of v1, /device:TPU:8, one launch (start us, length us, event | category | flops | bytes accessed | tf_op | source)
XLA Modules:
  0.0 441.0 jit_solution(1911743885842531731)
XLA Ops:
  6.5 0.0 reduce-scatter.2.cloned.1.call-start
  6.5 0.7 broadcast_in_dim.17
  7.3 0.1 reshape.19
  7.3 0.1 dynamic_slice.7
  7.4 14.0 %fusion.1 = f32[8192,512]{0,1:T(8,128)} fusion(bf16[512,512]{1,0:T(8,128)(2,1)} %param.7, bf16[512,8192]{1,0:T(8,128)(2,1)} %param.9, s32[8192]{0:T(1024)S(1)} %reshape.19, s32[512]{0:T(512)S(1)} %dynamic_slice.7), kind=kOutput, calls=%fused_computation.3 | convolution fusion | flops 4303355904 | bytes 25724928 | tf_op jit(solution)/shard_map/dot_general | solution.py:36
  21.4 0.0 copy-start
  21.4 0.0 reduce-scatter.2.cloned.1.call-update
  21.4 1.0 copy-done
  22.4 4.0 stack.2
  26.5 0.0 copy-start.1
  26.5 0.0 copy-start.2
  26.5 0.0 copy-start.3
  26.5 11.7 %all-to-all-start = ((bf16[16,512,512]{2,1,0:T(8,128)(2,1)}), bf16[16,512,512]{2,1,0:T(8,128)(2,1)}, u32[]{:S(2)}, u32[]{:S(2)}) async-start(bf16[16,512,512]{2,1,0:T(8,128)(2,1)} %stack.2), calls=%async_computation | async-start | bytes 16777216 | tf_op jit(solution)/shard_map/all_to_all | solution.py:11
  38.2 0.0 copy-done.1
  38.2 0.1 broadcast_in_dim.15
  38.3 0.1 reshape.17
  38.3 0.1 dynamic_slice.6
  38.4 182.4 %all-to-all-done = bf16[16,512,512]{2,1,0:T(8,128)(2,1)} async-done(((bf16[16,512,512]{2,1,0:T(8,128)(2,1)}), bf16[16,512,512]{2,1,0:T(8,128)(2,1)}, u32[]{:S(2)}, u32[]{:S(2)}) %all-to-all-start) | async-done | bytes 8388640 | tf_op jit(solution)/shard_map/all_to_all | solution.py:11
  220.8 201.5 %reduce-scatter.2.cloned.1.call-done = f32[512,512]{0,1:T(8,128)} async-done(((f32[8192,512]{0,1:T(8,128)}), f32[512,512]{0,1:T(8,128)}) %reduce-scatter.2.cloned.1.call-update) | async-done | bytes 1048592 | tf_op jit(solution)/shard_map/reduce_scatter | solution.py:35
  422.3 0.0 copy-done.2
  422.3 0.0 copy-done.3
  422.3 10.5 %subtract_divide_fusion = f32[512,512]{0,1:T(8,128)S(1)} fusion(f32[512,512]{0,1:T(8,128)} %reduce-scatter.2.cloned.1.call-done, bf16[8192,512]{1,0:T(8,128)(2,1)} %bitcast, bf16[512,8192]{1,0:T(8,128)(2,1)} %param.8, s32[8192]{0:T(1024)S(1)} %reshape.17, s32[512]{0:T(512)S(1)} %dynamic_slice.6, f32[512]{0:T(512)S(1)} %copy-done.2, f32[512]{0:T(512)S(1)} %copy-done.3), kind=kOutput, calls=%fused_computation.12 | convolution fusion | flops 4304142336 | bytes 18913280 | tf_op jit(solution)/shard_map/dot_general | solution.py:28
  432.9 1.3 copy.11
Async XLA Ops:
  6.5 415.8 %reduce-scatter.2.cloned.1.call-start = ((), (), s32[]{:S(2)}) async-start(), calls=%async_computation.2 | async-start | bytes 17825792 | tf_op jit(solution)/shard_map/reduce_scatter | solution.py:35
  21.4 1.0 copy-start
  26.5 11.7 %copy-start.1 = (s32[128]{0:T(128)S(1)}, s32[128]{0:T(128)}, u32[]{:S(2)}) copy-start(s32[128]{0:T(128)} %param.10) | copy-start | bytes 1540
  26.5 395.8 %copy-start.2 = (f32[512]{0:T(512)S(1)}, f32[512]{0:T(512)}, u32[]{:S(2)}) copy-start(f32[512]{0:T(512)} %param.12) | copy-start | bytes 6148
  26.5 395.8 %copy-start.3 = (f32[512]{0:T(512)S(1)}, f32[512]{0:T(512)}, u32[]{:S(2)}) copy-start(f32[512]{0:T(512)} %param.13) | copy-start | bytes 6148
  26.5 194.3 %all-to-all-start = ((bf16[16,512,512]{2,1,0:T(8,128)(2,1)}), bf16[16,512,512]{2,1,0:T(8,128)(2,1)}, u32[]{:S(2)}, u32[]{:S(2)}) async-start(bf16[16,512,512]{2,1,0:T(8,128)(2,1)} %stack.2), calls=%async_computation | async-start | bytes 16777216 | tf_op jit(solution)/shard_map/all_to_all | solution.py:11
Sparse Core Ops, SparseCore 0:
  21.5 400.7 reduce-scatter.1
